TPU v7x, 512 devices: a whole 4x8x8 slice. The times are simulated.
512 devices in a mesh: blk: 32 (over z_lo, y, core), rows: 16 (over x, z_hi).
Axes of the slice: x: 4, y: 8, z: 8 (z_hi: 4, z_lo: 2; z = z_hi * 2 + z_lo), core: 2. Of those that a mesh axis runs over, the one named last changes fastest.
Arguments:
- covariance: float32 [16384, 2, 32, 256], P('rows', None, 'blk'), may hold values from 0 to 5, as said below
- panel_order: int32 [64], replicated, may hold values from 0 to 63, each once
Outputs:
- factored: float32 [16384, 2, 32, 256], P('rows', None, 'blk')
Inputs may be any that keep to these rules, and one draw needn't show every extreme that they name: covariance is symmetric and positive definite. `panel_order`: every panel appears once; panel j is held by index j % 32 of blk.
All inputs are finite; a program needn't handle non-finite values.
Results may differ from a plain program's by a relative error of at most 0.0003.
Values sent between devices are 32-bit elements; how exact they have to be, the bound alone decides.
No kernel may reach another device: no remote copies, remote signals or barrier semaphores. Data moves between devices by JAX's collectives and lax.ppermute only.
A program may use at most 64 MiB of HBM per device.

v0:
```python
import jax
import jax.numpy as jnp
from jax import lax
from jax.sharding import PartitionSpec as P

SECTIONS = 2


def padded_to(lines, size):
    spare = -lines.shape[0] % size
    if not spare:
        return lines
    return jnp.concatenate([lines, jnp.zeros((spare, *lines.shape[1:]), lines.dtype)])


def broadcast_by_parts(array, axis, root):
    lines = jnp.where(lax.axis_index(axis) == root, array, jnp.zeros_like(array)).reshape(
        -1, *array.shape[1:][-1:]
    )
    padded = padded_to(lines, lax.axis_size(axis))
    own = lax.psum_scatter(padded, axis, scatter_dimension=0, tiled=True)
    return lax.all_gather(own, axis, axis=0, tiled=True)[: len(lines)].reshape(array.shape)


def from_root(array, axis, root):
    return lax.dynamic_index_in_dim(lax.all_gather(array, axis), root, 0, keepdims=False)


def inverse_factor(diagonal_block):
    lower_factor = jnp.linalg.cholesky(diagonal_block)
    identity_block = jnp.eye(diagonal_block.shape[0], dtype=diagonal_block.dtype)
    return lax.linalg.triangular_solve(lower_factor, identity_block, left_side=True, lower=True)


def product(first_matrix, second_matrix):
    return jnp.dot(
        first_matrix,
        second_matrix,
        precision=lax.Precision.HIGHEST,
        preferred_element_type=jnp.float32,
    )


def local(covariance, panel_order):
    row_count = covariance.shape[0]
    slot_count = covariance.shape[1]
    panel_width = covariance.shape[3]
    owner_count = lax.axis_size("blk")
    column_index = lax.axis_index("blk")
    row_index = lax.axis_index("rows")
    working = covariance.reshape(row_count, slot_count, panel_width)
    identity_block = jnp.eye(panel_width, dtype=jnp.float32)
    slot_panels = jnp.arange(slot_count, dtype=jnp.int32) * owner_count + column_index
    for round_index in range(SECTIONS):
        target = panel_order[round_index]
        owner_column = target % owner_count
        slot_here = target // owner_count
        first_column = target * panel_width
        root_row = first_column // row_count
        offset = first_column % row_count
        finished = jnp.any(slot_panels[:, None] == panel_order[None, : round_index + 1], axis=1)
        target_slot = slot_panels == target
        live_weight = jnp.where(finished, 0.0, 1.0).astype(jnp.float32)
        local_panel = lax.dynamic_index_in_dim(working, slot_here, 1, keepdims=False)
        received_panel = broadcast_by_parts(local_panel, "blk", owner_column)
        diagonal_block = lax.dynamic_slice_in_dim(received_panel, offset, panel_width, 0)
        diagonal_block = jnp.where(row_index == root_row, diagonal_block, identity_block)
        inverse = inverse_factor(diagonal_block)
        across = lax.dynamic_slice_in_dim(working, offset, panel_width, 0).reshape(
            panel_width, slot_count * panel_width
        )
        solved = product(inverse.T, product(inverse, across)).reshape(
            panel_width, slot_count, panel_width
        )
        solved = jnp.where(
            target_slot[None, :, None], inverse.T[:, None, :], solved * live_weight[None, :, None]
        )
        solved = from_root(solved, "rows", root_row)
        change = jnp.einsum(
            "rk,kpc->rpc",
            received_panel,
            solved,
            precision=lax.Precision.HIGHEST,
            preferred_element_type=jnp.float32,
        )
        working = jnp.where(target_slot[None, :, None], change, working - change)
    return working.reshape(row_count, slot_count, 1, panel_width)


def solution(mesh):
    return jax.shard_map(
        local,
        mesh=mesh,
        in_specs=(P("rows", None, "blk", None), P()),
        out_specs=P("rows", None, "blk", None),
        check_vma=False,
    )
```

profile of v0, /device:TPU:2, one launch (start us, length us, event | category | flops | bytes accessed | tf_op | source)
XLA Modules:
  0.0 798.6 jit_solution(15428723638569665150)
XLA Ops:
  6.5 1.3 fusion.42
  10.4 1.9 constant_dynamic-slice_fusion.5
  12.4 1.3 copy.57
  13.8 1.3 copy.53
  15.2 125.6 %reduce-scatter.7.cloned.1.call-done = f32[32,256]{1,0:T(8,128)} async-done(((f32[1024,256]{1,0:T(8,128)}), f32[32,256]{1,0:T(8,128)}) %reduce-scatter.7.cloned.1.call-update) | async-done | bytes 32784 | tf_op jit(solution)/shard_map/reduce_scatter | solution.py:21
  141.6 1.6 dynamic-slice_reduce_fusion
  143.9 60.9 %all-gather.5.cloned.1.call-done = f32[1024,256]{1,0:T(8,128)} async-done(((f32[32,256]{1,0:T(8,128)}), f32[1024,256]{1,0:T(8,128)}) %all-gather.5.cloned.1.call-update) | async-done | bytes 1048592 | tf_op jit(solution)/shard_map/all_gather | solution.py:22
  204.8 1.0 constant_dynamic-slice_fusion.4
  205.9 0.8 copy.35
  206.8 1.0 fusion.10
  207.8 0.7 copy-done.3
  208.5 11.7 %cholesky.130 = f32[128,128]{1,0:T(8,128)S(1)} custom-call(f32[128,128]{1,0:T(8,128)S(1)} %cholesky.194), custom_call_target="Cholesky" | custom-call | tf_op jit(solution)/shard_map/jit(cholesky)/cholesky | solution.py:30
  220.2 9.8 %custom-call.13 = f32[1,128,128]{1,2,0:T(8,128)S(1)} custom-call(f32[1,128,128]{2,1,0:T(8,128)S(1)} %get-tuple-element.52), custom_call_target="InvertDiagBlocksLowerTriangular" | custom-call | tf_op jit(solution)/shard_map/jit(cholesky)/cholesky | solution.py:30
  230.1 1.0 constant_dynamic-update-slice_fusion.1
  231.1 1.1 convolution_subtract_fusion.3
  232.2 12.2 %cholesky.147 = f32[128,128]{1,0:T(8,128)S(1)} custom-call(f32[128,128]{1,0:T(8,128)S(1)} %convolution_subtract_fusion.3), custom_call_target="Cholesky" | custom-call | tf_op jit(solution)/shard_map/jit(cholesky)/cholesky | solution.py:30
  244.4 0.7 compare_reduce_fusion.2
  246.6 4.0 while.4
  247.2 1.4 bitcast_dynamic-update-slice_fusion.4
  249.2 1.4 bitcast_dynamic-update-slice_fusion.4
  250.5 19.7 %custom-call.14 = f32[2,128,128]{1,2,0:T(8,128)S(1)} custom-call(f32[2,128,128]{2,1,0:T(8,128)S(1)} %get-tuple-element.21), custom_call_target="InvertDiagBlocksLowerTriangular" | custom-call | tf_op jit(solution)/shard_map/triangular_solve/custom-call.0 | solution.py:32
  271.3 0.7 fusion.19
  273.3 1.8 copy.37
  275.4 1.9 fusion.6
  279.6 4.4 copy.40
  284.1 116.5 %all-gather.7.cloned.1.call-done = f32[16,256,2,256]{3,1,2,0:T(8,128)} async-done(((f32[1,256,2,256]{3,1,2,0:T(8,128)}), f32[16,256,2,256]{3,1,2,0:T(8,128)}) %all-gather.7.cloned.1.call-update) | async-done | bytes 8388624 | tf_op jit(solution)/shard_map/all_gather | solution.py:26
  400.6 3.7 subtract_select_fusion.1
  404.4 1.3 copy.55
  405.8 118.6 %reduce-scatter.9.cloned.1.call-done = f32[32,256]{1,0:T(8,128)} async-done(((f32[1024,256]{1,0:T(8,128)}), f32[32,256]{1,0:T(8,128)}) %reduce-scatter.9.cloned.1.call-update) | async-done | bytes 32784 | tf_op jit(solution)/shard_map/reduce_scatter | solution.py:21
  526.1 62.1 %all-gather.9.cloned.1.call-done = f32[1024,256]{1,0:T(8,128)} async-done(((f32[32,256]{1,0:T(8,128)}), f32[1024,256]{1,0:T(8,128)}) %all-gather.9.cloned.1.call-update) | async-done | bytes 1048592 | tf_op jit(solution)/shard_map/all_gather | solution.py:22
  588.2 1.0 constant_dynamic-slice_fusion.3
  589.3 0.8 copy.43
  590.2 1.0 fusion.9
  591.2 0.7 copy-done.2
  591.9 11.7 %cholesky.164 = f32[128,128]{1,0:T(8,128)S(1)} custom-call(f32[128,128]{1,0:T(8,128)S(1)} %cholesky.197), custom_call_target="Cholesky" | custom-call | tf_op jit(solution)/shard_map/jit(cholesky)/cholesky | solution.py:30
  603.6 0.6 compare_reduce_fusion.1
  604.3 9.8 %custom-call.15 = f32[1,128,128]{1,2,0:T(8,128)S(1)} custom-call(f32[1,128,128]{2,1,0:T(8,128)S(1)} %get-tuple-element.48), custom_call_target="InvertDiagBlocksLowerTriangular" | custom-call | tf_op jit(solution)/shard_map/jit(cholesky)/cholesky | solution.py:30
  614.1 1.0 constant_dynamic-update-slice_fusion
  615.2 1.1 convolution_subtract_fusion.2
  616.3 11.7 %cholesky.181 = f32[128,128]{1,0:T(8,128)S(1)} custom-call(f32[128,128]{1,0:T(8,128)S(1)} %convolution_subtract_fusion.2), custom_call_target="Cholesky" | custom-call | tf_op jit(solution)/shard_map/jit(cholesky)/cholesky | solution.py:30
  629.9 4.0 while.5
  630.8 1.3 bitcast_dynamic-update-slice_fusion.5
  632.7 1.3 bitcast_dynamic-update-slice_fusion.5
  634.0 19.7 %custom-call.16 = f32[2,128,128]{1,2,0:T(8,128)S(1)} custom-call(f32[2,128,128]{2,1,0:T(8,128)S(1)} %get-tuple-element.22), custom_call_target="InvertDiagBlocksLowerTriangular" | custom-call | tf_op jit(solution)/shard_map/triangular_solve/custom-call.0 | solution.py:32
  656.5 0.9 fusion.5
  657.4 123.3 %all-gather.11.cloned.1.call-done = f32[16,256,2,256]{3,1,2,0:T(8,128)} async-done(((f32[1,256,2,256]{3,1,2,0:T(8,128)}), f32[16,256,2,256]{3,1,2,0:T(8,128)}) %all-gather.11.cloned.1.call-update) | async-done | bytes 8388624 | tf_op jit(solution)/shard_map/all_gather | solution.py:26
  780.8 4.7 fusion
  785.5 6.0 copy.49
  (71 shorter events, 11.3 us)
Async XLA Ops:
  6.5 134.3 %reduce-scatter.7.cloned.1.call-start = ((), (), s32[]{:S(2)}) async-start(), calls=%async_computation.6 | async-start | bytes 1081344 | tf_op jit(solution)/shard_map/reduce_scatter | solution.py:21
  13.8 127.7 %copy-start = (f32[1024,2,1,256]{3,2,1,0:T(1,128)S(1)}, f32[1024,2,1,256]{3,2,1,0:T(1,128)}, u32[]{:S(2)}) copy-start(f32[1024,2,1,256]{3,2,1,0:T(1,128)} %param.5) | copy-start | bytes 6291460
  15.2 189.6 %all-gather.5.cloned.1.call-start = ((), (), s32[]{:S(2)}) async-start(), calls=%async_computation.2 | async-start | bytes 1081344 | tf_op jit(solution)/shard_map/all_gather | solution.py:22
  140.9 259.7 %all-gather.7.cloned.1.call-start = ((), (), s32[]{:S(2)}) async-start(), calls=%async_computation.3 | async-start | bytes 8912896 | tf_op jit(solution)/shard_map/all_gather | solution.py:26
  207.8 0.7 copy-start.3
  277.3 247.1 %reduce-scatter.9.cloned.1.call-start = ((), (), s32[]{:S(2)}) async-start(), calls=%async_computation.7 | async-start | bytes 1081344 | tf_op jit(solution)/shard_map/reduce_scatter | solution.py:21
  279.6 121.0 %copy-start.1 = (f32[1024,256]{1,0:T(8,128)S(1)}, f32[1024,256]{1,0:T(8,128)}, u32[]{:S(2)}) copy-start(f32[1024,256]{1,0:T(8,128)} %all-gather.5.cloned.1.call-done) | copy-start | bytes 3145732
  404.4 121.4 %copy-start.4 = (s32[64]{0:T(128)S(1)}, s32[64]{0:T(128)}, u32[]{:S(2)}) copy-start(s32[64]{0:T(128)} %param.6) | copy-start | bytes 772
  405.8 182.4 %all-gather.9.cloned.1.call-start = ((), (), s32[]{:S(2)}) async-start(), calls=%async_computation.4 | async-start | bytes 1081344 | tf_op jit(solution)/shard_map/all_gather | solution.py:22
  524.4 256.3 %all-gather.11.cloned.1.call-start = ((), (), s32[]{:S(2)}) async-start(), calls=%async_computation.5 | async-start | bytes 8912896 | tf_op jit(solution)/shard_map/all_gather | solution.py:26
  591.2 0.7 copy-start.2
Sparse Core Ops, SparseCore 0:
  15.3 125.5 reduce-scatter.6
  143.0 61.7 all-gather.4
  277.4 123.1 all-gather.6
  405.9 118.4 reduce-scatter.8
  526.4 61.7 all-gather.8
  657.6 123.1 all-gather.10
where the time goes:
time: 809 us; the launch traced here: 799 us
  waiting for transfers between devices  607 us (75%)
  other arithmetic  116 us (14%)
  local copies, waits for them, and re-layouts  35 us (4%)
  between operations  22.8 us (3%)
  matrix products  17.2 us (2%)
    reduce_scatter x2, waiting for transfers between devices, broadcast_by_parts(): own = lax.psum_scatter(padded, axis, scatter_dimension=0, tiled=True)  244 us
    all_gather x2, waiting for transfers between devices, from_root(): lax.all_gather(array, axis)  240 us
    all_gather x2, waiting for transfers between devices, broadcast_by_parts(): lax.all_gather(own, axis, axis=0, tiled=True)[:len(lines)]  123 us
    another operation x13, other arithmetic, inverse_factor(): lower_factor = jnp.linalg.cholesky(diagonal_block)  69 us
    another operation x5, other arithmetic, inverse_factor(): lax.linalg.triangular_solve(lower_factor, identity_block, left_side=True,...  39.4 us
  transfers between devices with their start and end apart: 6, of which 6 were waited for; matrix products, arithmetic and copies ran while one was open for 1% of the time, Pallas kernels for 0%

commit v1 on v0

--- a/solution.py
+++ b/solution.py
@@ -2,6 +2,7 @@
 import jax.numpy as jnp
 from jax import lax
 from jax.sharding import PartitionSpec as P
+from jax.lax import all_to_all, axis_size
 
 SECTIONS = 2
 
@@ -19,7 +20,9 @@
     )
     padded = padded_to(lines, lax.axis_size(axis))
     own = lax.psum_scatter(padded, axis, scatter_dimension=0, tiled=True)
-    return lax.all_gather(own, axis, axis=0, tiled=True)[: len(lines)].reshape(array.shape)
+    return jnp.concatenate(all_to_all(jnp.stack([own] * axis_size(axis)), axis, 0, 0), axis=0)[
+        : len(lines)
+    ].reshape(array.shape)
 
 
 def from_root(array, axis, root):

time: 809 us -> 777 us (0.960)
  waiting for transfers between devices: 607 us -> 530 us
  local copies, waits for them, and re-layouts: 35 us -> 52.4 us
  other arithmetic: 116 us -> 128 us
    all_gather x2 -> x0, waiting for transfers between devices: 123 us -> none  [broadcast_by_parts(): lax.all_gather(own, axis, axis=0, tiled=True)[:len(lines)]]
    all_to_all x0 -> x2, waiting for transfers between devices: none -> 50.4 us  [broadcast_by_parts(): all_to_all(jnp.stack([own] * axis_size(axis)), axis, 0, 0)]
where the time goes in v1:
time: 777 us; the launch traced here: 766 us
  waiting for transfers between devices  530 us (68%)
  other arithmetic  128 us (16%)
  local copies, waits for them, and re-layouts  52.4 us (7%)
  matrix products  23.6 us (3%)
  between operations  22.9 us (3%)
  starting transfers between devices  8.16 us (1%)
    reduce_scatter x2, waiting for transfers between devices, broadcast_by_parts(): own = lax.psum_scatter(padded, axis, scatter_dimension=0, tiled=True)  244 us
    all_gather x2, waiting for transfers between devices, from_root(): lax.all_gather(array, axis)  235 us
    another operation x13, other arithmetic, inverse_factor(): lower_factor = jnp.linalg.cholesky(diagonal_block)  71.6 us
    all_to_all x2, waiting for transfers between devices, broadcast_by_parts(): all_to_all(jnp.stack([own] * axis_size(axis)), axis, 0, 0)  50.4 us
    another operation x5, other arithmetic, inverse_factor(): lax.linalg.triangular_solve(lower_factor, identity_block, left_side=True,...  44.3 us
  transfers between devices with their start and end apart: 6, of which 6 were waited for; matrix products, arithmetic and copies ran while one was open for 1% of the time, Pallas kernels for 0%

profile of v1, /device:TPU:2, one launch (start us, length us, event | category | flops | bytes accessed | tf_op | source)
XLA Modules:
  0.0 765.5 jit_solution(1754476759122427524)
XLA Ops:
  6.5 1.3 fusion.40
  10.7 2.1 broadcast_select_fusion
  13.9 125.7 %reduce-scatter.5.cloned.1.call-done = f32[32,256]{1,0:T(8,128)} async-done(((f32[1024,256]{1,0:T(8,128)}), f32[32,256]{1,0:T(8,128)}) %reduce-scatter.5.cloned.1.call-update) | async-done | bytes 32784 | tf_op jit(solution)/shard_map/reduce_scatter | solution.py:22
  139.5 1.8 stack.4
  141.4 3.9 all-to-all-start
  146.1 1.6 dynamic-slice_reduce_fusion
  149.3 24.5 %all-to-all-done = f32[32,32,256]{2,1,0:T(8,128)S(1)} async-done(((f32[32,32,256]{2,1,0:T(8,128)}), f32[32,32,256]{2,1,0:T(8,128)S(1)}, u32[]{:S(2)}, u32[]{:S(2)}) %all-to-all-start) | async-done | bytes 1048608 | tf_op jit(solution)/shard_map/all_to_all | solution.py:23
  174.5 1.8 copy.67
  177.0 1.8 copy.46
  180.5 11.7 %cholesky.130 = f32[128,128]{1,0:T(8,128)S(1)} custom-call(f32[128,128]{1,0:T(8,128)S(1)} %cholesky.194), custom_call_target="Cholesky" | custom-call | tf_op jit(solution)/shard_map/jit(cholesky)/cholesky | solution.py:33
  192.3 10.4 %custom-call.13 = f32[1,128,128]{1,2,0:T(8,128)} custom-call(f32[1,128,128]{2,1,0:T(8,128)S(1)} %get-tuple-element.52), custom_call_target="InvertDiagBlocksLowerTriangular" | custom-call | tf_op jit(solution)/shard_map/jit(cholesky)/cholesky | solution.py:33
  203.4 1.7 constant_dynamic-update-slice_fusion.1
  206.2 12.2 %cholesky.147 = f32[128,128]{1,0:T(8,128)S(1)} custom-call(f32[128,128]{1,0:T(8,128)S(1)} %convolution_subtract_fusion.3), custom_call_target="Cholesky" | custom-call | tf_op jit(solution)/shard_map/jit(cholesky)/cholesky | solution.py:33
  221.0 1.7 select_select_fusion.1
  222.8 5.8 while.4
  223.5 2.3 bitcast_dynamic-update-slice_fusion.4
  226.4 2.2 bitcast_dynamic-update-slice_fusion.4
  229.3 20.5 %custom-call.14 = f32[2,128,128]{1,2,0:T(8,128)S(1)} custom-call(f32[2,128,128]{2,1,0:T(8,128)} %copy-done.4), custom_call_target="InvertDiagBlocksLowerTriangular" | custom-call | tf_op jit(solution)/shard_map/triangular_solve/custom-call.0 | solution.py:35
  252.4 1.7 fusion.16
  254.1 1.4 fusion.15
  255.5 1.8 copy.48
  257.3 2.2 reshape.118
  259.4 2.1 fusion.4
  264.2 4.4 copy.51
  268.6 113.8 %all-gather.3.cloned.1.call-done = f32[16,256,2,256]{3,1,2,0:T(8,128)} async-done(((f32[1,256,2,256]{3,1,2,0:T(8,128)}), f32[16,256,2,256]{3,1,2,0:T(8,128)}) %all-gather.3.cloned.1.call-update) | async-done | bytes 8388624 | tf_op jit(solution)/shard_map/all_gather | solution.py:29
  382.4 3.7 subtract_select_fusion.1
  387.5 118.6 %reduce-scatter.7.cloned.1.call-done = f32[32,256]{1,0:T(8,128)} async-done(((f32[1024,256]{1,0:T(8,128)}), f32[32,256]{1,0:T(8,128)}) %reduce-scatter.7.cloned.1.call-update) | async-done | bytes 32784 | tf_op jit(solution)/shard_map/reduce_scatter | solution.py:22
  506.2 1.8 stack.5
  508.0 3.9 all-to-all-start.1
  514.6 25.9 %all-to-all-done.1 = f32[32,32,256]{2,1,0:T(8,128)S(1)} async-done(((f32[32,32,256]{2,1,0:T(8,128)}), f32[32,32,256]{2,1,0:T(8,128)S(1)}, u32[]{:S(2)}, u32[]{:S(2)}) %all-to-all-start.1) | async-done | bytes 1048608 | tf_op jit(solution)/shard_map/all_to_all | solution.py:23
  541.1 1.8 copy.68
  543.7 1.8 copy.54
  547.2 11.7 %cholesky.164 = f32[128,128]{1,0:T(8,128)S(1)} custom-call(f32[128,128]{1,0:T(8,128)S(1)} %cholesky.197), custom_call_target="Cholesky" | custom-call | tf_op jit(solution)/shard_map/jit(cholesky)/cholesky | solution.py:33
  559.6 10.4 %custom-call.15 = f32[1,128,128]{1,2,0:T(8,128)} custom-call(f32[1,128,128]{2,1,0:T(8,128)S(1)} %get-tuple-element.48), custom_call_target="InvertDiagBlocksLowerTriangular" | custom-call | tf_op jit(solution)/shard_map/jit(cholesky)/cholesky | solution.py:33
  570.7 1.7 constant_dynamic-update-slice_fusion
  573.5 11.7 %cholesky.181 = f32[128,128]{1,0:T(8,128)S(1)} custom-call(f32[128,128]{1,0:T(8,128)S(1)} %convolution_subtract_fusion.2), custom_call_target="Cholesky" | custom-call | tf_op jit(solution)/shard_map/jit(cholesky)/cholesky | solution.py:33
  587.8 1.7 select_select_fusion
  589.5 6.1 while.5
  590.5 2.3 bitcast_dynamic-update-slice_fusion.5
  593.4 2.2 bitcast_dynamic-update-slice_fusion.5
  596.3 20.5 %custom-call.16 = f32[2,128,128]{1,2,0:T(8,128)S(1)} custom-call(f32[2,128,128]{2,1,0:T(8,128)} %copy-done.3), custom_call_target="InvertDiagBlocksLowerTriangular" | custom-call | tf_op jit(solution)/shard_map/triangular_solve/custom-call.0 | solution.py:35
  618.7 1.7 fusion.13
  620.3 1.4 fusion.12
  622.6 2.2 reshape.122
  624.8 2.0 fusion.3
  626.8 121.6 %all-gather.5.cloned.1.call-done = f32[16,256,2,256]{3,1,2,0:T(8,128)} async-done(((f32[1,256,2,256]{3,1,2,0:T(8,128)}), f32[16,256,2,256]{3,1,2,0:T(8,128)}) %all-gather.5.cloned.1.call-update) | async-done | bytes 8388624 | tf_op jit(solution)/shard_map/all_gather | solution.py:29
  748.4 4.4 fusion
  752.7 6.0 copy.60
  (71 shorter events, 28.8 us)
Async XLA Ops:
  6.5 133.0 %reduce-scatter.5.cloned.1.call-start = ((), (), s32[]{:S(2)}) async-start(), calls=%async_computation.4 | async-start | bytes 1081344 | tf_op jit(solution)/shard_map/reduce_scatter | solution.py:22
  13.9 132.2 %copy-start = (f32[1024,2,1,256]{3,2,1,0:T(1,128)S(1)}, f32[1024,2,1,256]{3,2,1,0:T(1,128)}, u32[]{:S(2)}) copy-start(f32[1024,2,1,256]{3,2,1,0:T(1,128)} %param.5) | copy-start | bytes 6291460
  141.4 32.4 %all-to-all-start = ((f32[32,32,256]{2,1,0:T(8,128)}), f32[32,32,256]{2,1,0:T(8,128)S(1)}, u32[]{:S(2)}, u32[]{:S(2)}) async-start(f32[32,32,256]{2,1,0:T(8,128)} %stack.4), calls=%async_computation.1 | async-start | bytes 2097152 | tf_op jit(solution)/shard_map/all_to_all | solution.py:23
  145.3 237.1 %all-gather.3.cloned.1.call-start = ((), (), s32[]{:S(2)}) async-start(), calls=%async_computation.5 | async-start | bytes 8912896 | tf_op jit(solution)/shard_map/all_gather | solution.py:29
  179.8 0.7 copy-start.2
  228.6 0.7 copy-start.4
  261.5 244.6 %reduce-scatter.7.cloned.1.call-start = ((), (), s32[]{:S(2)}) async-start(), calls=%async_computation.7 | async-start | bytes 1081344 | tf_op jit(solution)/shard_map/reduce_scatter | solution.py:22
  387.5 126.0 %copy-start.5 = (s32[64]{0:T(128)S(1)}, s32[64]{0:T(128)}, u32[]{:S(2)}) copy-start(s32[64]{0:T(128)} %param.6) | copy-start | bytes 772
  508.0 32.4 %all-to-all-start.1 = ((f32[32,32,256]{2,1,0:T(8,128)}), f32[32,32,256]{2,1,0:T(8,128)S(1)}, u32[]{:S(2)}, u32[]{:S(2)}) async-start(f32[32,32,256]{2,1,0:T(8,128)} %stack.5), calls=%async_computation.2 | async-start | bytes 2097152 | tf_op jit(solution)/shard_map/all_to_all | solution.py:23
  512.0 236.4 %all-gather.5.cloned.1.call-start = ((), (), s32[]{:S(2)}) async-start(), calls=%async_computation.6 | async-start | bytes 8912896 | tf_op jit(solution)/shard_map/all_gather | solution.py:29
  546.5 0.7 copy-start.1
  595.6 0.7 copy-start.3
Sparse Core Ops, SparseCore 0:
  14.0 125.5 reduce-scatter.4
  261.7 120.6 all-gather.2
  387.7 118.4 reduce-scatter.6
  626.9 121.3 all-gather.4
